TPU v7x, 32 devices: a whole 2x2x4 slice. The times are simulated.
32 devices in a mesh: st: 8 (over z, x), gr: 4 (over y, core).
Axes of the slice: x: 2, y: 2, z: 4, core: 2. Of those that a mesh axis runs over, the one named last changes fastest.
Arguments:
- states: float32 [32, 24, 768], P(('st', 'gr')), may hold values from -6 to 6
- regions: int32 [24, 768], replicated, may hold values from 0 to 7
- pot_table: float32 [8], replicated, may hold values from -3 to 0
- subspace: bfloat16 [32, 32], P(None, 'st'), may hold values from -1.5 to 1.5
- state_order: int32 [32], replicated, may hold values from 0 to 31, each once
Outputs:
- rotated: bfloat16 [32, 24, 768], P('st', 'gr')
Inputs may be any that keep to these rules, and one draw needn't show every extreme that they name: state_order is a permutation of the window positions.
All inputs are finite; a program needn't handle non-finite values.
Results may differ from a plain program's by a relative error of at most 0.0049.
Values may be sent and summed in bfloat16 or wider, within the bound.
No kernel may reach another device: no remote copies, remote signals or barrier semaphores. Data moves between devices by JAX's collectives and lax.ppermute only.
A program may use at most 64 MiB of HBM per device.

v0:
```python
import jax
import jax.numpy as jnp
from jax import lax
from jax.sharding import PartitionSpec as P

NY = 24
NZ = 32
DEG = 4
coef_center = -5369.0 / 1800.0
coef_list = (12.0 / 7.0, -15.0 / 56.0, 10.0 / 189.0, -1.0 / 112.0, 2.0 / 1925.0, -1.0 / 16632.0)
centre = 6.75
half_width = 5.25


def shift_cols(field, offset):
    width = field.shape[1]
    if offset > 0:
        return jnp.pad(field[:, offset:], ((0, 0), (0, offset)))
    return jnp.pad(field[:, : width + offset], ((0, 0), (-offset, 0)))


def shift_rows(field, offset):
    height = field.shape[0]
    if offset > 0:
        return jnp.pad(field[offset:, :], ((0, offset), (0, 0)))
    return jnp.pad(field[: height + offset, :], ((-offset, 0), (0, 0)))


def laplace(field):
    zpos = lax.broadcasted_iota(jnp.int32, field.shape, 1) % NZ
    total = 3.0 * coef_center * field
    for step in range(1, 7):
        xpair = shift_rows(field, step) + shift_rows(field, -step)
        ypair = shift_cols(field, step * NZ) + shift_cols(field, -step * NZ)
        zplus = jnp.where(zpos + step < NZ, shift_cols(field, step), 0.0)
        zminus = jnp.where(zpos - step >= 0, shift_cols(field, -step), 0.0)
        total = total + coef_list[step - 1] * (xpair + ypair + (zplus + zminus))
    return total


def shifted_op(field, potential):
    return -0.5 * laplace(field) + potential * field - centre * field


def lookup(regions, pot_table):
    levels = lax.broadcasted_iota(jnp.int32, (pot_table.shape[0], 1, 1), 0)
    hits = regions[None, :, :] == levels
    return jnp.sum(jnp.where(hits, pot_table[:, None, None], 0.0), axis=0)


def per_device(states, regions, pot_table, subspace, state_order):
    potential = lookup(regions, pot_table)
    previous = states[0]
    current = shifted_op(previous, potential) * (1.0 / half_width)
    for step in range(1, DEG):
        following = shifted_op(current, potential) * (2.0 / half_width) - previous
        previous = current
        current = following
    filtered = current.astype(jnp.bfloat16)
    groups = lax.axis_size("gr")
    weights = jnp.take(subspace, state_order, axis=0)
    columns = weights.shape[1]
    blocks = lax.all_to_all(filtered[None], "gr", split_axis=1, concat_axis=0, tiled=True)
    slab_rows = blocks.shape[1]
    flat_blocks = blocks.reshape(groups, slab_rows * NY * NZ)
    summed = lax.dot_general(
        weights,
        lax.all_gather(flat_blocks, "st", axis=0, tiled=True),
        (((0,), (0,)), ((), ())),
        preferred_element_type=jnp.float32,
    )
    return summed.reshape(columns, slab_rows, NY * NZ).astype(jnp.bfloat16)


def solution(mesh):
    in_specs = (P(("st", "gr"), None, None), P(), P(), P(None, "st"), P())
    out_specs = P("st", "gr", None)
    return jax.shard_map(
        per_device, mesh=mesh, in_specs=in_specs, out_specs=out_specs, check_vma=False
    )
```

profile of v0, /device:TPU:0, one launch (start us, length us, event | category | flops | bytes accessed | tf_op | source)
XLA Modules:
  0.0 51.4 jit_solution(2509546299188329413)
XLA Ops:
  0.0 1.1 %fusion.75 = (f32[24,736]{1,0:T(8,128)S(1)}, f32[24,736]{1,0:T(8,128)S(1)}) fusion(f32[24,768]{1,0:T(8,128)} %bitcast.37), kind=kLoop, calls=%fused_computation.112 | loop fusion | bytes 282624 | tf_op jit(solution)/shard_map/slice | solution.py:18
  1.2 0.1 fusion.77
  1.3 0.1 fusion.78
  1.3 0.1 fusion.79
  1.4 0.1 fusion.80
  1.5 0.1 fusion.82
  1.6 0.1 fusion.84
  1.7 0.1 fusion.86
  2.1 0.8 %copy-done.1 = s32[24,768]{1,0:T(8,128)S(1)} copy-done((s32[24,768]{1,0:T(8,128)S(1)}, s32[24,768]{1,0:T(8,128)}, u32[]{:S(2)}) %copy-start.1) | copy-done | bytes 73752
  3.0 0.1 select_reduce_fusion
  3.1 0.4 broadcast_multiply_fusion
  3.9 0.1 fusion.59
  4.1 0.1 fusion.62
  4.3 0.1 fusion.65
  4.6 0.4 multiply_subtract_fusion.1
  5.4 0.1 fusion.44
  5.5 0.1 fusion.47
  6.1 0.4 multiply_subtract_fusion
  6.7 0.1 fusion.23
  6.9 0.1 fusion.26
  7.7 0.4 fusion.12
  8.2 0.5 broadcast.651
  8.7 0.8 %reduce.2 = bf16[24,768]{1,0:T(8,128)(2,1)S(1)} reduce(bf16[24,1,768]{2,1,0:T(2,128)(2,1)S(1)} %bitcast.49, bf16[]{:T(256)} %broadcast.651), dimensions={1}, to_apply=%bitcast.36.reduce_sub_computation | reduce | bytes 73730
  9.5 0.6 %reshape.42 = bf16[4,2,2304]{2,1,0:T(2,128)(2,1)} reshape(bf16[24,768]{1,0:T(8,128)(2,1)S(1)} %reduce.2) | data formatting | bytes 73728
  10.2 4.4 %all-to-all-start = ((bf16[4,2,2304]{2,1,0:T(2,128)(2,1)}), bf16[4,2,2304]{2,1,0:T(2,128)(2,1)S(1)}, u32[]{:S(2)}, u32[]{:S(2)}) async-start(bf16[4,2,2304]{2,1,0:T(2,128)(2,1)} %reshape.42), calls=%async_computation | async-start | bytes 73728 | tf_op jit(solution)/shard_map/all_to_all | solution.py:63
  14.6 0.7 %copy-done.2 = bf16[32,4]{0,1:T(4,128)(2,1)S(1)} copy-done((bf16[32,4]{0,1:T(4,128)(2,1)S(1)}, bf16[32,4]{0,1:T(4,128)(2,1)}, u32[]{:S(2)}) %copy-start.2) | copy-done | bytes 280
  15.3 0.1 copy.15
  15.4 0.6 %gather_fusion = bf16[32,4]{1,0:T(8,128)(2,1)S(1)} fusion(bf16[32,4]{1,0:T(8,128)(2,1)S(1)} %copy.15, s32[1024]{0:T(1024)S(1)} %pad_clamp_fusion), kind=kCustom, calls=%fused_computation | custom fusion | bytes 640 | tf_op jit(solution)/shard_map/jit(_take)/gather | solution.py:61
  16.0 2.6 %all-to-all-done = bf16[4,2,2304]{2,1,0:T(2,128)(2,1)S(1)} async-done(((bf16[4,2,2304]{2,1,0:T(2,128)(2,1)}), bf16[4,2,2304]{2,1,0:T(2,128)(2,1)S(1)}, u32[]{:S(2)}, u32[]{:S(2)}) %all-to-all-start) | async-done | bytes 36896 | tf_op jit(solution)/shard_map/all_to_all | solution.py:63
  18.6 0.2 bitcast_reduce_fusion
  18.8 31.6 %all-gather = bf16[8,4,4608]{2,1,0:T(4,128)(2,1)S(1)} all-gather(bf16[1,4,4608]{2,1,0:T(4,128)(2,1)S(1)} %reshape.38), channel_id=1, replica_groups=mesh['st'=8,'gr'=4] {'st'}, dimensions={0}, use_global_device_ids=true | all-gather | bytes 331776 | tf_op jit(solution)/shard_map/all_gather | solution.py:68
  50.5 0.9 %convolution_convert_fusion = bf16[4,4608]{1,0:T(4,128)(2,1)} fusion(bf16[32,4608]{1,0:T(8,128)(2,1)S(1)} %reshape.39, bf16[32,4]{1,0:T(8,128)(2,1)S(1)} %gather_fusion, pred[32]{0:T(512)(128)(4,1)S(1)} %compare_and_fusion), kind=kOutput, calls=%fused_computation.1 | convolution fusion | flops 1198208 | bytes 332064 | tf_op jit(solution)/shard_map/dot_general | solution.py:66
  (74 shorter events, 3.0 us)
Async XLA Ops:
  0.0 1.1 %copy-start = (f32[1,24,768]{2,1,0:T(8,128)S(1)}, f32[1,24,768]{2,1,0:T(8,128)}, u32[]{:S(2)}) copy-start(f32[1,24,768]{2,1,0:T(8,128)} %param.5) | copy-start | bytes 221188
  2.1 0.9 %copy-start.1 = (s32[24,768]{1,0:T(8,128)S(1)}, s32[24,768]{1,0:T(8,128)}, u32[]{:S(2)}) copy-start(s32[24,768]{1,0:T(8,128)} %param.6) | copy-start | bytes 221188
  2.1 0.9 %copy-start.3 = (f32[8]{0:T(128)S(1)}, f32[8]{0:T(128)}, u32[]{:S(2)}) copy-start(f32[8]{0:T(128)} %param.7) | copy-start | bytes 100
  10.2 4.4 %copy-start.4 = (s32[32]{0:T(128)S(1)}, s32[32]{0:T(128)}, u32[]{:S(2)}) copy-start(s32[32]{0:T(128)} %param.9) | copy-start | bytes 388
  10.2 8.4 %all-to-all-start = ((bf16[4,2,2304]{2,1,0:T(2,128)(2,1)}), bf16[4,2,2304]{2,1,0:T(2,128)(2,1)S(1)}, u32[]{:S(2)}, u32[]{:S(2)}) async-start(bf16[4,2,2304]{2,1,0:T(2,128)(2,1)} %reshape.42), calls=%async_computation | async-start | bytes 73728 | tf_op jit(solution)/shard_map/all_to_all | solution.py:63
  14.6 0.7 %copy-start.2 = (bf16[32,4]{0,1:T(4,128)(2,1)S(1)}, bf16[32,4]{0,1:T(4,128)(2,1)}, u32[]{:S(2)}) copy-start(bf16[32,4]{0,1:T(4,128)(2,1)} %param.8) | copy-start | bytes 772
where the time goes:
time: 51.7 us; the launch traced here: 51.4 us
  blocking collectives  31.6 us (61%)
  local copies, waits for them, and re-layouts  8.8 us (17%)
  starting transfers between devices  4.4 us (9%)
  other arithmetic  2.71 us (5%)
  waiting for transfers between devices  2.57 us (5%)
  matrix products  0.91 us (2%)
    all_gather x1, blocking collectives, per_device(): lax.all_gather(flat_blocks, 'st', axis=0, tiled=True)  31.6 us
    slice x48, local copies, waits for them, and re-layouts, shift_cols(): return jnp.pad(field[:, offset:], ((0, 0), (0, offset)))  4.65 us
    all_to_all x1, starting transfers between devices, per_device(): lax.all_to_all(filtered[None], 'gr', split_axis=1, concat_axis=0, tiled=T...  4.4 us
    unnamed x16, local copies, waits for them, and re-layouts  2.9 us
    all_to_all x1, waiting for transfers between devices, per_device(): lax.all_to_all(filtered[None], 'gr', split_axis=1, concat_axis=0, tiled=T...  2.57 us
  transfers between devices with their start and end apart: 1, of which 1 were waited for; matrix products, arithmetic and copies ran while one was open for 1% of the time, Pallas kernels for 0%

commit v1 on v0

--- a/solution.py
+++ b/solution.py
@@ -10,6 +10,27 @@
 coef_list = (12.0 / 7.0, -15.0 / 56.0, 10.0 / 189.0, -1.0 / 112.0, 2.0 / 1925.0, -1.0 / 16632.0)
 centre = 6.75
 half_width = 5.25
+
+
+def collect(value, axis, dim):
+    devices, here, span = (lax.axis_size(axis), lax.axis_index(axis), value.shape[dim])
+    ahead = [(i, (i + 1) % devices) for i in range(devices)]
+    left = [(i, (i - 1) % devices) for i in range(devices)]
+    out = jnp.zeros((*value.shape[:dim], devices * span, *value.shape[dim + 1 :]), value.dtype)
+    out = lax.dynamic_update_slice_in_dim(out, value, here * span, axis=dim)
+    from_left = from_right = value
+    half = devices // 2
+    for hop in range(1, half + 1):
+        from_left = lax.ppermute(from_left, axis, ahead)
+        out = lax.dynamic_update_slice_in_dim(
+            out, from_left, (here - hop) % devices * span, axis=dim
+        )
+        if hop < devices - half:
+            from_right = lax.ppermute(from_right, axis, left)
+            out = lax.dynamic_update_slice_in_dim(
+                out, from_right, (here + hop) % devices * span, axis=dim
+            )
+    return out
 
 
 def shift_cols(field, offset):
@@ -65,7 +86,7 @@
     flat_blocks = blocks.reshape(groups, slab_rows * NY * NZ)
     summed = lax.dot_general(
         weights,
-        lax.all_gather(flat_blocks, "st", axis=0, tiled=True),
+        collect(flat_blocks, "st", 0),
         (((0,), (0,)), ((), ())),
         preferred_element_type=jnp.float32,
     )

time: 51.7 us -> 47 us (0.909)
  blocking collectives: 31.6 us -> 0 us
  starting transfers between devices: 4.4 us -> 19.1 us
  waiting for transfers between devices: 2.57 us -> 14.4 us
    all_gather x1 -> x0, blocking collectives: 31.6 us -> none  [per_device(): lax.all_gather(flat_blocks, 'st', axis=0, tiled=True)]
    ppermute x0 -> x7, starting transfers between devices: none -> 14.7 us  [the longest x3 12.7 us: collect(): from_right = lax.ppermute(from_right, axis, left)]
    ppermute x0 -> x7, waiting for transfers between devices: none -> 12 us  [the longest x4 12 us: collect(): from_left = lax.ppermute(from_left, axis, ahead)]
    unnamed x16 -> x14, local copies, waits for them, and re-layouts: 2.9 us -> 2.82 us
  transfers between devices with their start and end apart: 1 -> 8, of which waited for: 1 -> 5; matrix products, arithmetic and copies ran while one was open for 1% -> 2% of each run, Pallas kernels for 0% -> 0%
where the time goes in v1:
time: 47 us; the launch traced here: 46.7 us
  starting transfers between devices  19.1 us (41%)
  waiting for transfers between devices  14.4 us (31%)
  local copies, waits for them, and re-layouts  9.01 us (19%)
  other arithmetic  2.71 us (6%)
  matrix products  0.91 us (2%)
  between operations  0.56 us (1%)
    ppermute x3, starting transfers between devices, collect(): from_right = lax.ppermute(from_right, axis, left)  12.7 us
    ppermute x4, waiting for transfers between devices, collect(): from_left = lax.ppermute(from_left, axis, ahead)  12 us
    slice x48, local copies, waits for them, and re-layouts, shift_cols(): return jnp.pad(field[:, offset:], ((0, 0), (0, offset)))  4.65 us
    all_to_all x1, starting transfers between devices, per_device(): lax.all_to_all(filtered[None], 'gr', split_axis=1, concat_axis=0, tiled=T...  4.4 us
    unnamed x14, local copies, waits for them, and re-layouts  2.82 us
    all_to_all x1, waiting for transfers between devices, per_device(): lax.all_to_all(filtered[None], 'gr', split_axis=1, concat_axis=0, tiled=T...  2.44 us
    ppermute x4, starting transfers between devices, collect(): from_left = lax.ppermute(from_left, axis, ahead)  2 us
  transfers between devices with their start and end apart: 8, of which 5 were waited for; matrix products, arithmetic and copies ran while one was open for 2% of the time, Pallas kernels for 0%

profile of v1, /device:TPU:0, one launch (start us, length us, event | category | flops | bytes accessed | tf_op | source)
XLA Modules:
  0.0 46.7 jit_solution(6913393524318438423)
XLA Ops:
  0.0 1.1 %fusion.75 = (f32[24,736]{1,0:T(8,128)S(1)}, f32[24,736]{1,0:T(8,128)S(1)}) fusion(f32[24,768]{1,0:T(8,128)} %bitcast.37), kind=kLoop, calls=%fused_computation.120 | loop fusion | bytes 282624 | tf_op jit(solution)/shard_map/slice | solution.py:39
  1.3 0.1 fusion.78
  1.3 0.1 fusion.79
  1.4 0.1 fusion.80
  1.5 0.1 fusion.82
  1.6 0.1 fusion.84
  1.7 0.1 fusion.86
  2.1 0.8 %copy-done.1 = s32[24,768]{1,0:T(8,128)S(1)} copy-done((s32[24,768]{1,0:T(8,128)S(1)}, s32[24,768]{1,0:T(8,128)}, u32[]{:S(2)}) %copy-start.1) | copy-done | bytes 73752
  3.0 0.1 select_reduce_fusion
  3.1 0.4 broadcast_multiply_fusion
  3.9 0.1 fusion.59
  4.6 0.4 multiply_subtract_fusion.1
  6.1 0.4 multiply_subtract_fusion
  7.7 0.4 fusion.12
  8.2 0.5 %broadcast.658 = bf16[]{:T(256)} broadcast(bf16[]{:T(256)} %constant.517), dimensions={} | broadcast | bytes 4
  8.7 0.8 %reduce.2 = bf16[24,768]{1,0:T(8,128)(2,1)S(1)} reduce(bf16[24,1,768]{2,1,0:T(2,128)(2,1)S(1)} %bitcast.49, bf16[]{:T(256)} %broadcast.658), dimensions={1}, to_apply=%bitcast.36.reduce_sub_computation | reduce | bytes 73730
  9.5 0.6 %reshape.39 = bf16[4,2,2304]{2,1,0:T(2,128)(2,1)} reshape(bf16[24,768]{1,0:T(8,128)(2,1)S(1)} %reduce.2) | data formatting | bytes 73728
  10.2 4.4 %all-to-all-start = ((bf16[4,2,2304]{2,1,0:T(2,128)(2,1)}), bf16[4,2,2304]{2,1,0:T(2,128)(2,1)S(1)}, u32[]{:S(2)}, u32[]{:S(2)}) async-start(bf16[4,2,2304]{2,1,0:T(2,128)(2,1)} %reshape.39), calls=%async_computation | async-start | bytes 73728 | tf_op jit(solution)/shard_map/all_to_all | solution.py:84
  14.7 0.7 %copy-done.2 = bf16[32,4]{0,1:T(4,128)(2,1)S(1)} copy-done((bf16[32,4]{0,1:T(4,128)(2,1)S(1)}, bf16[32,4]{0,1:T(4,128)(2,1)}, u32[]{:S(2)}) %copy-start.2) | copy-done | bytes 280
  15.4 0.1 copy.15
  15.5 0.6 %gather_fusion = bf16[32,4]{1,0:T(8,128)(2,1)S(1)} fusion(bf16[32,4]{1,0:T(8,128)(2,1)S(1)} %copy.15, s32[1024]{0:T(1024)S(1)} %pad_clamp_fusion), kind=kCustom, calls=%fused_computation | custom fusion | bytes 640 | tf_op jit(solution)/shard_map/jit(_take)/gather | solution.py:82
  16.1 2.4 %all-to-all-done = bf16[4,2,2304]{2,1,0:T(2,128)(2,1)S(1)} async-done(((bf16[4,2,2304]{2,1,0:T(2,128)(2,1)}), bf16[4,2,2304]{2,1,0:T(2,128)(2,1)S(1)}, u32[]{:S(2)}, u32[]{:S(2)}) %all-to-all-start) | async-done | bytes 36896 | tf_op jit(solution)/shard_map/all_to_all | solution.py:84
  18.6 0.2 bitcast_reduce_fusion
  18.8 2.0 %collective-permute-start = (bf16[4,4608]{1,0:T(4,128)(2,1)S(1)}, bf16[4,4608]{1,0:T(4,128)(2,1)S(1)}, u32[]{:S(2)}, u32[]{:S(2)}) collective-permute-start(bf16[4,4608]{1,0:T(4,128)(2,1)S(1)} %reshape.28), channel_id=1, source_target_pairs={{0,4},{4,8},{8,12},{12,16},{16,20},{20,24},{24,28},{28,0},{1,5},{5... | collective-permute-start | bytes 110600 | tf_op jit(solution)/shard_map/ppermute | solution.py:24
  20.8 3.1 %collective-permute-start.1 = (bf16[4,4608]{1,0:T(4,128)(2,1)S(1)}, bf16[4,4608]{1,0:T(4,128)(2,1)S(1)}, u32[]{:S(2)}, u32[]{:S(2)}) collective-permute-start(bf16[4,4608]{1,0:T(4,128)(2,1)S(1)} %reshape.28), channel_id=1, source_target_pairs={{0,28},{4,0},{8,4},{12,8},{16,12},{20,16},{24,20},{28,24},{1,29},{... | collective-permute-start | bytes 110600 | tf_op jit(solution)/shard_map/ppermute | solution.py:29
  24.0 1.8 %collective-permute-done = bf16[4,4608]{1,0:T(4,128)(2,1)S(1)} collective-permute-done((bf16[4,4608]{1,0:T(4,128)(2,1)S(1)}, bf16[4,4608]{1,0:T(4,128)(2,1)S(1)}, u32[]{:S(2)}, u32[]{:S(2)}) %collective-permute-start) | collective-permute-done | bytes 36896 | tf_op jit(solution)/shard_map/ppermute | solution.py:24
  25.8 4.8 %collective-permute-start.3 = (bf16[4,4608]{1,0:T(4,128)(2,1)S(1)}, bf16[4,4608]{1,0:T(4,128)(2,1)S(1)}, u32[]{:S(2)}, u32[]{:S(2)}) collective-permute-start(bf16[4,4608]{1,0:T(4,128)(2,1)S(1)} %collective-permute-done.1), channel_id=1, source_target_pairs={{0,28},{4,0},{8,4},{12,8},{16,12},{20,16},{24,20},{28,24},{1,29},{... | collective-permute-start | bytes 110600 | tf_op jit(solution)/shard_map/ppermute | solution.py:29
  30.6 1.8 %collective-permute-done.2 = bf16[4,4608]{1,0:T(4,128)(2,1)S(1)} collective-permute-done((bf16[4,4608]{1,0:T(4,128)(2,1)S(1)}, bf16[4,4608]{1,0:T(4,128)(2,1)S(1)}, u32[]{:S(2)}, u32[]{:S(2)}) %collective-permute-start.2) | collective-permute-done | bytes 36896 | tf_op jit(solution)/shard_map/ppermute | solution.py:24
  32.4 4.8 %collective-permute-start.5 = (bf16[4,4608]{1,0:T(4,128)(2,1)S(1)}, bf16[4,4608]{1,0:T(4,128)(2,1)S(1)}, u32[]{:S(2)}, u32[]{:S(2)}) collective-permute-start(bf16[4,4608]{1,0:T(4,128)(2,1)S(1)} %collective-permute-done.3), channel_id=1, source_target_pairs={{0,28},{4,0},{8,4},{12,8},{16,12},{20,16},{24,20},{28,24},{1,29},{... | collective-permute-start | bytes 110600 | tf_op jit(solution)/shard_map/ppermute | solution.py:29
  37.3 1.8 %collective-permute-done.4 = bf16[4,4608]{1,0:T(4,128)(2,1)S(1)} collective-permute-done((bf16[4,4608]{1,0:T(4,128)(2,1)S(1)}, bf16[4,4608]{1,0:T(4,128)(2,1)S(1)}, u32[]{:S(2)}, u32[]{:S(2)}) %collective-permute-start.4) | collective-permute-done | bytes 36896 | tf_op jit(solution)/shard_map/ppermute | solution.py:24
  39.2 6.6 %collective-permute-done.6 = bf16[4,4608]{1,0:T(4,128)(2,1)S(1)} collective-permute-done((bf16[4,4608]{1,0:T(4,128)(2,1)S(1)}, bf16[4,4608]{1,0:T(4,128)(2,1)S(1)}, u32[]{:S(2)}, u32[]{:S(2)}) %collective-permute-start.6) | collective-permute-done | bytes 36896 | tf_op jit(solution)/shard_map/ppermute | solution.py:24
  45.8 0.9 %convolution_convert_fusion = bf16[4,4608]{1,0:T(4,128)(2,1)} fusion(bf16[32,4608]{1,0:T(8,128)(2,1)S(1)} %constant_dynamic-update-slice_fusion, bf16[32,4]{1,0:T(8,128)(2,1)S(1)} %gather_fusion, pred[32]{0:T(512)(128)(4,1)S(1)} %compare_and_fusion), kind=kOutput, calls=%fused_computation.1 | convolution fusion | flops 1198208 | bytes 332064 | tf_op jit(solution)/shard_map/dot_general | solution.py:87
  (95 shorter events, 3.8 us)
Async XLA Ops:
  0.0 1.1 %copy-start = (f32[1,24,768]{2,1,0:T(8,128)S(1)}, f32[1,24,768]{2,1,0:T(8,128)}, u32[]{:S(2)}) copy-start(f32[1,24,768]{2,1,0:T(8,128)} %param.5) | copy-start | bytes 221188
  2.1 0.9 %copy-start.1 = (s32[24,768]{1,0:T(8,128)S(1)}, s32[24,768]{1,0:T(8,128)}, u32[]{:S(2)}) copy-start(s32[24,768]{1,0:T(8,128)} %param.6) | copy-start | bytes 221188
  2.1 0.9 %copy-start.3 = (f32[8]{0:T(128)S(1)}, f32[8]{0:T(128)}, u32[]{:S(2)}) copy-start(f32[8]{0:T(128)} %param.7) | copy-start | bytes 100
  10.2 4.4 %copy-start.4 = (s32[32]{0:T(128)S(1)}, s32[32]{0:T(128)}, u32[]{:S(2)}) copy-start(s32[32]{0:T(128)} %param.9) | copy-start | bytes 388
  10.2 8.4 %all-to-all-start = ((bf16[4,2,2304]{2,1,0:T(2,128)(2,1)}), bf16[4,2,2304]{2,1,0:T(2,128)(2,1)S(1)}, u32[]{:S(2)}, u32[]{:S(2)}) async-start(bf16[4,2,2304]{2,1,0:T(2,128)(2,1)} %reshape.39), calls=%async_computation | async-start | bytes 73728 | tf_op jit(solution)/shard_map/all_to_all | solution.py:84
  14.7 0.7 %copy-start.2 = (bf16[32,4]{0,1:T(4,128)(2,1)S(1)}, bf16[32,4]{0,1:T(4,128)(2,1)}, u32[]{:S(2)}) copy-start(bf16[32,4]{0,1:T(4,128)(2,1)} %param.8) | copy-start | bytes 772
  18.8 7.0 %collective-permute-start = (bf16[4,4608]{1,0:T(4,128)(2,1)S(1)}, bf16[4,4608]{1,0:T(4,128)(2,1)S(1)}, u32[]{:S(2)}, u32[]{:S(2)}) collective-permute-start(bf16[4,4608]{1,0:T(4,128)(2,1)S(1)} %reshape.28), channel_id=1, source_target_pairs={{0,4},{4,8},{8,12},{12,16},{16,20},{20,24},{24,28},{28,0},{1,5},{5... | collective-permute-start | bytes 110600 | tf_op jit(solution)/shard_map/ppermute | solution.py:24
  20.8 5.0 %collective-permute-start.1 = (bf16[4,4608]{1,0:T(4,128)(2,1)S(1)}, bf16[4,4608]{1,0:T(4,128)(2,1)S(1)}, u32[]{:S(2)}, u32[]{:S(2)}) collective-permute-start(bf16[4,4608]{1,0:T(4,128)(2,1)S(1)} %reshape.28), channel_id=1, source_target_pairs={{0,28},{4,0},{8,4},{12,8},{16,12},{20,16},{24,20},{28,24},{1,29},{... | collective-permute-start | bytes 110600 | tf_op jit(solution)/shard_map/ppermute | solution.py:29
  25.8 6.7 %collective-permute-start.2 = (bf16[4,4608]{1,0:T(4,128)(2,1)S(1)}, bf16[4,4608]{1,0:T(4,128)(2,1)S(1)}, u32[]{:S(2)}, u32[]{:S(2)}) collective-permute-start(bf16[4,4608]{1,0:T(4,128)(2,1)S(1)} %collective-permute-done), channel_id=1, source_target_pairs={{0,4},{4,8},{8,12},{12,16},{16,20},{20,24},{24,28},{28,0},{1,5},{5... | collective-permute-start | bytes 110600 | tf_op jit(solution)/shard_map/ppermute | solution.py:24
  25.8 6.7 %collective-permute-start.3 = (bf16[4,4608]{1,0:T(4,128)(2,1)S(1)}, bf16[4,4608]{1,0:T(4,128)(2,1)S(1)}, u32[]{:S(2)}, u32[]{:S(2)}) collective-permute-start(bf16[4,4608]{1,0:T(4,128)(2,1)S(1)} %collective-permute-done.1), channel_id=1, source_target_pairs={{0,28},{4,0},{8,4},{12,8},{16,12},{20,16},{24,20},{28,24},{1,29},{... | collective-permute-start | bytes 110600 | tf_op jit(solution)/shard_map/ppermute | solution.py:29
  32.4 6.7 %collective-permute-start.4 = (bf16[4,4608]{1,0:T(4,128)(2,1)S(1)}, bf16[4,4608]{1,0:T(4,128)(2,1)S(1)}, u32[]{:S(2)}, u32[]{:S(2)}) collective-permute-start(bf16[4,4608]{1,0:T(4,128)(2,1)S(1)} %collective-permute-done.2), channel_id=1, source_target_pairs={{0,4},{4,8},{8,12},{12,16},{16,20},{20,24},{24,28},{28,0},{1,5},{5... | collective-permute-start | bytes 110600 | tf_op jit(solution)/shard_map/ppermute | solution.py:24
  32.4 6.7 %collective-permute-start.5 = (bf16[4,4608]{1,0:T(4,128)(2,1)S(1)}, bf16[4,4608]{1,0:T(4,128)(2,1)S(1)}, u32[]{:S(2)}, u32[]{:S(2)}) collective-permute-start(bf16[4,4608]{1,0:T(4,128)(2,1)S(1)} %collective-permute-done.3), channel_id=1, source_target_pairs={{0,28},{4,0},{8,4},{12,8},{16,12},{20,16},{24,20},{28,24},{1,29},{... | collective-permute-start | bytes 110600 | tf_op jit(solution)/shard_map/ppermute | solution.py:29
  39.1 6.7 %collective-permute-start.6 = (bf16[4,4608]{1,0:T(4,128)(2,1)S(1)}, bf16[4,4608]{1,0:T(4,128)(2,1)S(1)}, u32[]{:S(2)}, u32[]{:S(2)}) collective-permute-start(bf16[4,4608]{1,0:T(4,128)(2,1)S(1)} %collective-permute-done.4), channel_id=1, source_target_pairs={{0,4},{4,8},{8,12},{12,16},{16,20},{20,24},{24,28},{28,0},{1,5},{5... | collective-permute-start | bytes 110600 | tf_op jit(solution)/shard_map/ppermute | solution.py:24
